TPU v7x, 32 devices: a whole 2x2x4 slice. The times are simulated.
32 devices in a mesh: fsdp: 2 (over x), ctx: 4 (over z), tp: 4 (over y, core).
Axes of the slice: x: 2, y: 2, z: 4, core: 2. Of those that a mesh axis runs over, the one named last changes fastest.
Arguments:
- tokens: bfloat16 [4, 1024, 2048], P('fsdp', 'ctx'), may hold values from -36 to 36
- cotangent: bfloat16 [4, 1024, 2048], P('fsdp', 'ctx'), may hold values from -9 to 9
- lengths: int32 [4, 2], P('fsdp'), may hold values from 1 to 768, 1024 in all within a row
- deal: int32 [4, 1024], P('fsdp'), may hold values from 0 to 1023, each once within a row
- att_proj: float32 [3, 2048, 2048], P(None, ('fsdp', 'ctx'), 'tp'), may hold values from -0.125 to 0.125
- attn_out: float32 [2048, 2048], P(('fsdp', 'ctx'), 'tp'), may hold values from -0.75 to 0.75
- ff_proj: float32 [2, 2048, 8192], P(None, ('fsdp', 'ctx'), 'tp'), may hold values from -0.125 to 0.125
- ff_out: float32 [2048, 8192], P(('fsdp', 'ctx'), 'tp'), may hold values from -0.0625 to 0.0625
- att_proj_first: float32 [3, 2048, 2048], P(None, ('fsdp', 'ctx'), 'tp')
- attn_out_first: float32 [2048, 2048], P(('fsdp', 'ctx'), 'tp')
- ff_proj_first: float32 [2, 2048, 8192], P(None, ('fsdp', 'ctx'), 'tp')
- ff_out_first: float32 [2048, 8192], P(('fsdp', 'ctx'), 'tp')
- att_proj_second: float32 [3, 2048, 2048], P(None, ('fsdp', 'ctx'), 'tp'), as said below
- attn_out_second: float32 [2048, 2048], P(('fsdp', 'ctx'), 'tp'), as said below
- ff_proj_second: float32 [2, 2048, 8192], P(None, ('fsdp', 'ctx'), 'tp'), as said below
- ff_out_second: float32 [2048, 8192], P(('fsdp', 'ctx'), 'tp'), as said below
Outputs:
- block_out: bfloat16 [4, 1024, 2048], P('fsdp', 'ctx')
- input_grad: float32 [4, 1024, 2048], P('fsdp', 'ctx')
- grad_norm: float32 [1], replicated
- att_proj_grad: float32 [3, 2048, 2048], P(None, ('fsdp', 'ctx'), 'tp')
- attn_out_grad: float32 [2048, 2048], P(('fsdp', 'ctx'), 'tp')
- ff_proj_grad: float32 [2, 2048, 8192], P(None, ('fsdp', 'ctx'), 'tp')
- ff_out_grad: float32 [2048, 8192], P(('fsdp', 'ctx'), 'tp')
- att_proj_first_new: float32 [3, 2048, 2048], P(None, ('fsdp', 'ctx'), 'tp')
- attn_out_first_new: float32 [2048, 2048], P(('fsdp', 'ctx'), 'tp')
- ff_proj_first_new: float32 [2, 2048, 8192], P(None, ('fsdp', 'ctx'), 'tp')
- ff_out_first_new: float32 [2048, 8192], P(('fsdp', 'ctx'), 'tp')
- att_proj_second_new: float32 [3, 2048, 2048], P(None, ('fsdp', 'ctx'), 'tp')
- attn_out_second_new: float32 [2048, 2048], P(('fsdp', 'ctx'), 'tp')
- ff_proj_second_new: float32 [2, 2048, 8192], P(None, ('fsdp', 'ctx'), 'tp')
- ff_out_second_new: float32 [2048, 8192], P(('fsdp', 'ctx'), 'tp')
- att_proj_new: float32 [3, 2048, 2048], P(None, ('fsdp', 'ctx'), 'tp')
- attn_out_new: float32 [2048, 2048], P(('fsdp', 'ctx'), 'tp')
- ff_proj_new: float32 [2, 2048, 8192], P(None, ('fsdp', 'ctx'), 'tp')
- ff_out_new: float32 [2048, 8192], P(('fsdp', 'ctx'), 'tp')
- att_proj_low: bfloat16 [3, 2048, 2048], P(None, ('fsdp', 'ctx'), 'tp')
- attn_out_low: bfloat16 [2048, 2048], P(('fsdp', 'ctx'), 'tp')
- ff_proj_low: bfloat16 [2, 2048, 8192], P(None, ('fsdp', 'ctx'), 'tp')
- ff_out_low: bfloat16 [2048, 8192], P(('fsdp', 'ctx'), 'tp')
Inputs may be any that keep to these rules, and one draw needn't show every extreme that they name: `lengths`: each row sums to 1024 and no entry exceeds 768. `deal`: each row is a permutation of the positions of its pack. `att_proj_second`: every entry is positive. `attn_out_second`: every entry is positive. `ff_proj_second`: every entry is positive. `ff_out_second`: every entry is positive.
All inputs are finite; a program needn't handle non-finite values.
Results may differ from a plain program's by a relative error of at most 0.017.
Values may be sent and summed in bfloat16 or wider, within the bound.
A program may use at most 320 MiB of HBM per device.

v0:
```python
import jax
import jax.numpy as jnp
from jax import lax
from jax.sharding import PartitionSpec as P

D = 2048
HEAD_DIM = 128
STEP = 10
EPS_NORM = 1e-05
BETA_ONE = 0.9
BETA_TWO = 0.95
EPS_ADAM = 1e-08
DECAY = 0.1
MAX_NORM = 1.0
NEG_FILL = -1e30


def layer_norm(values):
    centre = values - jnp.mean(values, axis=-1, keepdims=True)
    spread = jnp.mean(centre * centre, axis=-1, keepdims=True)
    return centre * lax.rsqrt(spread + EPS_NORM)


def rotary(values, cos_table, sine_table):
    half_dim = values.shape[-1] // 2
    turned = jnp.concatenate([-values[..., half_dim:], values[..., :half_dim]], axis=-1)
    return values * cos_table + turned * sine_table


def rope_tables(places):
    freq_steps = jnp.arange(HEAD_DIM // 2, dtype=jnp.float32)
    inverse = jnp.power(10000.0, -2.0 * freq_steps / HEAD_DIM)
    angles = places.astype(jnp.float32)[:, None] * inverse[None, :]
    doubled = jnp.concatenate([angles, angles], axis=1)
    return (jnp.cos(doubled)[:, None, :], jnp.sin(doubled)[:, None, :])


def first_positions(deal_row, length_row):
    seq_ends = jnp.cumsum(length_row)
    starts = seq_ends - length_row
    inside = (deal_row[:, None] >= starts[None, :]) & (deal_row[:, None] < seq_ends[None, :])
    return jnp.sum(jnp.where(inside, starts[None, :], 0), axis=1)


def swiglu(gate_up):
    return gate_up[1] * jax.nn.sigmoid(gate_up[1]) * gate_up[0]


def adam_step(weight, grad_sum, first, second, clip_factor, learn_rate):
    clipped = grad_sum * clip_factor
    first_new = BETA_ONE * first + (1.0 - BETA_ONE) * clipped
    second_new = BETA_TWO * second + (1.0 - BETA_TWO) * clipped * clipped
    first_hat = first_new / (1.0 - BETA_ONE**STEP)
    second_hat = second_new / (1.0 - BETA_TWO**STEP)
    weight_new = weight - learn_rate * (
        first_hat / (jnp.sqrt(second_hat) + EPS_ADAM) + DECAY * weight
    )
    return (first_new, second_new, weight_new)


def tensor_sum(partial_sum):
    return lax.psum(partial_sum, "tp")


def gather_weights(att_proj, attn_out, ff_proj, ff_out):
    att_full, proj_full = (
        lax.all_gather(att_proj.astype(jnp.bfloat16), ("fsdp", "ctx"), axis=1, tiled=True),
        lax.all_gather(ff_proj.astype(jnp.bfloat16), ("fsdp", "ctx"), axis=1, tiled=True),
    )
    out_full, down_full = (
        lax.all_gather(attn_out.astype(jnp.bfloat16), ("fsdp", "ctx"), axis=0, tiled=True),
        lax.all_gather(ff_out.astype(jnp.bfloat16), ("fsdp", "ctx"), axis=0, tiled=True),
    )
    return (att_full, out_full, proj_full, down_full)


def reduce_grads(att_grad, out_grad, proj_grad, down_grad):
    att_part, proj_part = (
        lax.psum_scatter(
            att_grad.astype(jnp.bfloat16), ("fsdp", "ctx"), scatter_dimension=1, tiled=True
        ).astype(jnp.float32),
        lax.psum_scatter(
            proj_grad.astype(jnp.bfloat16), ("fsdp", "ctx"), scatter_dimension=1, tiled=True
        ).astype(jnp.float32),
    )
    out_part, down_part = (
        lax.psum_scatter(
            out_grad.astype(jnp.bfloat16), ("fsdp", "ctx"), scatter_dimension=0, tiled=True
        ).astype(jnp.float32),
        lax.psum_scatter(
            down_grad.astype(jnp.bfloat16), ("fsdp", "ctx"), scatter_dimension=0, tiled=True
        ).astype(jnp.float32),
    )
    return (att_part, out_part, proj_part, down_part)


def micro_step(resid_in, grad_out, deal_row, length_row, weights, ctx_index):
    att_full, out_full, proj_full, down_full = weights
    row_count = resid_in.shape[0]
    head_width = att_full.shape[2]
    local_heads = head_width // HEAD_DIM
    score_scale = HEAD_DIM ** (-0.5)
    key_first = first_positions(deal_row, length_row)
    query_place = lax.dynamic_slice_in_dim(deal_row, ctx_index * row_count, row_count)
    query_first = lax.dynamic_slice_in_dim(key_first, ctx_index * row_count, row_count)
    allowed = (deal_row[None, :] <= query_place[:, None]) & (
        deal_row[None, :] >= query_first[:, None]
    )
    cos_table, sine_table = rope_tables(query_place - query_first)
    normed_one, norm_one_pull = jax.vjp(layer_norm, resid_in)
    act_one = normed_one.astype(jnp.bfloat16)
    joint_qkv = jnp.einsum("td,cdf->ctf", act_one, att_full, preferred_element_type=jnp.float32)

    def turn_pair(query_raw, key_raw):
        return (rotary(query_raw, cos_table, sine_table), rotary(key_raw, cos_table, sine_table))

    (query_rot, key_rot), turn_pull = jax.vjp(
        turn_pair,
        joint_qkv[0].reshape(row_count, local_heads, HEAD_DIM),
        joint_qkv[1].reshape(row_count, local_heads, HEAD_DIM),
    )
    query_low = query_rot.astype(jnp.bfloat16)
    key_low = key_rot.reshape(row_count, head_width).astype(jnp.bfloat16)
    value_low = joint_qkv[2].astype(jnp.bfloat16)
    keys_flat, values_flat = (
        lax.all_gather(key_low, "ctx", axis=0, tiled=True),
        lax.all_gather(value_low, "ctx", axis=0, tiled=True),
    )
    pack_len = keys_flat.shape[0]
    keys_all = keys_flat.reshape(pack_len, local_heads, HEAD_DIM)
    values_all = values_flat.reshape(pack_len, local_heads, HEAD_DIM)

    def scores_of():
        raw_scores = (
            jnp.einsum("thd,khd->htk", query_low, keys_all, preferred_element_type=jnp.float32)
            * score_scale
        )
        return jnp.where(allowed[None], raw_scores, NEG_FILL)

    scores = scores_of()
    row_peak = jnp.max(scores, axis=2, keepdims=True)
    exp_scores = jnp.exp(scores - row_peak)
    row_mass = jnp.sum(exp_scores, axis=2, keepdims=True)
    log_mass = row_peak + jnp.log(row_mass)
    attended = jnp.einsum(
        "htk,khd->thd",
        (exp_scores / row_mass).astype(jnp.bfloat16),
        values_all,
        preferred_element_type=jnp.float32,
    )
    attended_low = attended.reshape(row_count, head_width).astype(jnp.bfloat16)
    attn_branch = tensor_sum(
        jnp.einsum("tf,df->td", attended_low, out_full, preferred_element_type=jnp.float32)
    )
    resid_mid = resid_in + attn_branch
    normed_two, norm_two_pull = jax.vjp(layer_norm, resid_mid)
    act_two = normed_two.astype(jnp.bfloat16)
    gate_up = jnp.einsum("td,cdf->ctf", act_two, proj_full, preferred_element_type=jnp.float32)
    hidden, glu_pull = jax.vjp(swiglu, gate_up)
    hidden_low = hidden.astype(jnp.bfloat16)
    ff_branch = tensor_sum(
        jnp.einsum("tf,df->td", hidden_low, down_full, preferred_element_type=jnp.float32)
    )
    block_rows = (resid_mid + ff_branch).astype(jnp.bfloat16)
    down_grad = jnp.einsum("td,tf->df", grad_out, hidden_low, preferred_element_type=jnp.float32)
    hidden_grad = jnp.einsum("td,df->tf", grad_out, down_full, preferred_element_type=jnp.float32)
    (gate_up_grad,) = glu_pull(hidden_grad)
    gate_up_low = gate_up_grad.astype(jnp.bfloat16)
    proj_grad = jnp.einsum("td,ctf->cdf", act_two, gate_up_low, preferred_element_type=jnp.float32)
    act_two_grad = tensor_sum(
        jnp.einsum("ctf,cdf->td", gate_up_low, proj_full, preferred_element_type=jnp.float32)
    )
    (mid_back,) = norm_two_pull(act_two_grad)
    mid_grad = mid_back + grad_out.astype(jnp.float32)
    mid_low = mid_grad.astype(jnp.bfloat16)
    out_grad = jnp.einsum("td,tf->df", mid_low, attended_low, preferred_element_type=jnp.float32)
    attended_grad = jnp.einsum("td,df->tf", mid_low, out_full, preferred_element_type=jnp.float32)
    attended_grad = attended_grad.astype(jnp.bfloat16).reshape(row_count, local_heads, HEAD_DIM)
    scores = scores_of()
    probs = jnp.exp(scores - log_mass)
    value_grad = jnp.einsum(
        "htk,thd->khd",
        probs.astype(jnp.bfloat16),
        attended_grad,
        preferred_element_type=jnp.float32,
    )
    prob_grad = jnp.einsum(
        "thd,khd->htk", attended_grad, values_all, preferred_element_type=jnp.float32
    )
    delta_rows = jnp.sum(probs * prob_grad, axis=2, keepdims=True)
    score_grad = (probs * (prob_grad - delta_rows)).astype(jnp.bfloat16)
    query_grad = (
        jnp.einsum("htk,khd->thd", score_grad, keys_all, preferred_element_type=jnp.float32)
        * score_scale
    )
    key_grad = (
        jnp.einsum("htk,thd->khd", score_grad, query_low, preferred_element_type=jnp.float32)
        * score_scale
    )
    key_mine, value_mine = (
        lax.psum_scatter(
            key_grad.reshape(pack_len, head_width), "ctx", scatter_dimension=0, tiled=True
        ),
        lax.psum_scatter(
            value_grad.reshape(pack_len, head_width), "ctx", scatter_dimension=0, tiled=True
        ),
    )
    query_raw_grad, key_raw_grad = turn_pull(
        (query_grad, key_mine.reshape(row_count, local_heads, HEAD_DIM))
    )
    joint_grad = jnp.stack(
        [
            query_raw_grad.reshape(row_count, head_width),
            key_raw_grad.reshape(row_count, head_width),
            value_mine,
        ]
    ).astype(jnp.bfloat16)
    att_grad = jnp.einsum("td,ctf->cdf", act_one, joint_grad, preferred_element_type=jnp.float32)
    act_one_grad = tensor_sum(
        jnp.einsum("ctf,cdf->td", joint_grad, att_full, preferred_element_type=jnp.float32)
    )
    (in_back,) = norm_one_pull(act_one_grad)
    input_grad = in_back + mid_grad
    return (block_rows, input_grad, (att_grad, out_grad, proj_grad, down_grad))


def shards(
    tokens,
    cotangent,
    lengths,
    deal,
    att_proj,
    attn_out,
    ff_proj,
    ff_out,
    att_proj_first,
    attn_out_first,
    ff_proj_first,
    ff_out_first,
    att_proj_second,
    attn_out_second,
    ff_proj_second,
    ff_out_second,
):
    ctx_index = lax.axis_index("ctx")
    micro_count = tokens.shape[0]
    block_list = []
    input_list = []
    totals = None
    for batch_slot in range(micro_count):
        weights = gather_weights(att_proj, attn_out, ff_proj, ff_out)
        block_rows, input_grad, local_grads = micro_step(
            tokens[batch_slot].astype(jnp.float32),
            cotangent[batch_slot],
            deal[batch_slot],
            lengths[batch_slot],
            weights,
            ctx_index,
        )
        block_list.append(block_rows)
        input_list.append(input_grad)
        step_grads = reduce_grads(local_grads[0], local_grads[1], local_grads[2], local_grads[3])
        if batch_slot == 0:
            totals = step_grads
        else:
            totals = jax.tree.map(jnp.add, totals, step_grads)
    att_total, out_total, proj_total, down_total = totals
    square_sums = lax.psum(
        (
            jnp.sum(att_total * att_total),
            jnp.sum(out_total * out_total),
            jnp.sum(proj_total * proj_total),
            jnp.sum(down_total * down_total),
        ),
        ("fsdp", "ctx", "tp"),
    )
    norm_value = jnp.sqrt(square_sums[0] + square_sums[1] + square_sums[2] + square_sums[3])
    clip_factor = jnp.minimum(1.0, MAX_NORM / (norm_value + 1e-06))
    base_rate = D ** (-0.5)
    out_rate = (D // 32) ** (-0.5)
    att_first_new, att_second_new, att_new = adam_step(
        att_proj, att_total, att_proj_first, att_proj_second, clip_factor, base_rate
    )
    out_first_new, out_second_new, out_new = adam_step(
        attn_out, out_total, attn_out_first, attn_out_second, clip_factor, out_rate
    )
    proj_first_new, proj_second_new, proj_new = adam_step(
        ff_proj, proj_total, ff_proj_first, ff_proj_second, clip_factor, base_rate
    )
    down_first_new, down_second_new, down_new = adam_step(
        ff_out, down_total, ff_out_first, ff_out_second, clip_factor, base_rate
    )
    return (
        jnp.stack(block_list),
        jnp.stack(input_list),
        norm_value.reshape(1),
        att_total,
        out_total,
        proj_total,
        down_total,
        att_first_new,
        out_first_new,
        proj_first_new,
        down_first_new,
        att_second_new,
        out_second_new,
        proj_second_new,
        down_second_new,
        att_new,
        out_new,
        proj_new,
        down_new,
        att_new.astype(jnp.bfloat16),
        out_new.astype(jnp.bfloat16),
        proj_new.astype(jnp.bfloat16),
        down_new.astype(jnp.bfloat16),
    )


def solution(mesh):
    in_specs = (
        P("fsdp", "ctx", None),
        P("fsdp", "ctx", None),
        P("fsdp", None),
        P("fsdp", None),
        P(None, ("fsdp", "ctx"), "tp"),
        P(("fsdp", "ctx"), "tp"),
        P(None, ("fsdp", "ctx"), "tp"),
        P(("fsdp", "ctx"), "tp"),
        P(None, ("fsdp", "ctx"), "tp"),
        P(("fsdp", "ctx"), "tp"),
        P(None, ("fsdp", "ctx"), "tp"),
        P(("fsdp", "ctx"), "tp"),
        P(None, ("fsdp", "ctx"), "tp"),
        P(("fsdp", "ctx"), "tp"),
        P(None, ("fsdp", "ctx"), "tp"),
        P(("fsdp", "ctx"), "tp"),
    )
    out_specs = (
        P("fsdp", "ctx", None),
        P("fsdp", "ctx", None),
        P(),
        P(None, ("fsdp", "ctx"), "tp"),
        P(("fsdp", "ctx"), "tp"),
        P(None, ("fsdp", "ctx"), "tp"),
        P(("fsdp", "ctx"), "tp"),
        P(None, ("fsdp", "ctx"), "tp"),
        P(("fsdp", "ctx"), "tp"),
        P(None, ("fsdp", "ctx"), "tp"),
        P(("fsdp", "ctx"), "tp"),
        P(None, ("fsdp", "ctx"), "tp"),
        P(("fsdp", "ctx"), "tp"),
        P(None, ("fsdp", "ctx"), "tp"),
        P(("fsdp", "ctx"), "tp"),
        P(None, ("fsdp", "ctx"), "tp"),
        P(("fsdp", "ctx"), "tp"),
        P(None, ("fsdp", "ctx"), "tp"),
        P(("fsdp", "ctx"), "tp"),
        P(None, ("fsdp", "ctx"), "tp"),
        P(("fsdp", "ctx"), "tp"),
        P(None, ("fsdp", "ctx"), "tp"),
        P(("fsdp", "ctx"), "tp"),
    )
    return jax.shard_map(shards, mesh=mesh, in_specs=in_specs, out_specs=out_specs, check_vma=False)
```

profile of v0, /device:TPU:0, one launch (start us, length us, event | category | flops | bytes accessed | tf_op | source)
XLA Modules:
  0.0 2617.0 jit_solution(11051854917980619340)
XLA Ops:
  14.9 97.6 %all-gather.11.cloned.1.call-done = bf16[3,2048,512]{2,1,0:T(8,128)(2,1)} async-done(((bf16[3,256,512]{2,1,0:T(8,128)(2,1)}), bf16[3,2048,512]{2,1,0:T(8,128)(2,1)}) %all-gather.11.cloned.1.call-update) | async-done | bytes 6291472 | tf_op jit(solution)/shard_map/all_gather | solution.py:67
  112.5 4.6 convolution_bitcast_fusion.6
  132.8 4.8 convolution_bitcast_fusion.7
  148.3 5.8 all-gather.21.cloned.1.call-done
  155.6 28.1 %all-gather.25.cloned.1.call-done = bf16[1,1024,512]{2,1,0:T(8,128)(2,1)} async-done(((bf16[1,256,512]{2,1,0:T(8,128)(2,1)}), bf16[1,1024,512]{2,1,0:T(8,128)(2,1)}) %all-gather.25.cloned.1.call-update) | async-done | bytes 1048592 | tf_op jit(solution)/shard_map/all_gather | solution.py:127
  185.1 28.1 %all-gather.13.cloned.1.call-done = bf16[1024,512]{1,0:T(8,128)(2,1)} async-done(((bf16[256,512]{1,0:T(8,128)(2,1)}), bf16[1024,512]{1,0:T(8,128)(2,1)}) %all-gather.13.cloned.1.call-update) | async-done | bytes 1048592 | tf_op jit(solution)/shard_map/all_gather | solution.py:126
  214.7 27.9 %all-gather.23.cloned.1.call-done = bf16[1,1024,512]{2,1,0:T(8,128)(2,1)} async-done(((bf16[1,256,512]{2,1,0:T(8,128)(2,1)}), bf16[1,1024,512]{2,1,0:T(8,128)(2,1)}) %all-gather.23.cloned.1.call-update) | async-done | bytes 1048592 | tf_op jit(solution)/shard_map/all_gather | solution.py:127
  253.3 40.7 %all-gather.15.cloned.1.call-done = bf16[2048,512]{1,0:T(8,128)(2,1)} async-done(((bf16[256,512]{1,0:T(8,128)(2,1)}), bf16[2048,512]{1,0:T(8,128)(2,1)}) %all-gather.15.cloned.1.call-update) | async-done | bytes 2097168 | tf_op jit(solution)/shard_map/all_gather | solution.py:71
  294.0 3.8 fusion.144
  300.0 3.8 convert_element_type.242
  307.0 77.2 %all-reduce.25.cloned.1.call-done = (f32[256,2048]{1,0:T(8,128)}, f32[256,2048]{1,0:T(8,128)}) async-done(((f32[256,2048]{1,0:T(8,128)}, f32[256,2048]{1,0:T(8,128)}), (f32[256,2048]{1,0:T(8,128)}, f32[256,2048]{1,0:T(8,128)})) %all-reduce.25.cloned.1.call-update) | async-done | bytes 4194320 | tf_op jit(solution)/shard_map/psum | solution.py:62
  384.3 3.4 fusion.126
  389.5 225.4 %all-gather.17.cloned.1.call-done = bf16[2,2048,2048]{2,1,0:T(8,128)(2,1)} async-done(((bf16[2,256,2048]{2,1,0:T(8,128)(2,1)}), bf16[2,2048,2048]{2,1,0:T(8,128)(2,1)}) %all-gather.17.cloned.1.call-update) | async-done | bytes 16777232 | tf_op jit(solution)/shard_map/all_gather | solution.py:68
  615.0 13.2 convolution_bitcast_fusion
  628.1 6.3 convolution_bitcast_fusion.1
  634.4 106.6 %all-gather.19.cloned.1.call-done = bf16[2048,2048]{1,0:T(8,128)(2,1)} async-done(((bf16[256,2048]{1,0:T(8,128)(2,1)}), bf16[2048,2048]{1,0:T(8,128)(2,1)}) %all-gather.19.cloned.1.call-update) | async-done | bytes 8388624 | tf_op jit(solution)/shard_map/all_gather | solution.py:72
  741.0 10.6 multiply_bitcast_fusion.1
  751.6 5.9 multiply_bitcast_fusion.3
  757.5 13.5 convolution_bitcast_fusion.4
  771.0 13.9 convolution_bitcast_fusion.5
  785.7 83.3 %all-reduce.23.cloned.1.call-done = (f32[256,2048]{1,0:T(8,128)}, f32[256,2048]{1,0:T(8,128)}) async-done(((f32[256,2048]{1,0:T(8,128)}, f32[256,2048]{1,0:T(8,128)}), (f32[256,2048]{1,0:T(8,128)}, f32[256,2048]{1,0:T(8,128)})) %all-reduce.23.cloned.1.call-update) | async-done | bytes 4194320 | tf_op jit(solution)/shard_map/psum | solution.py:62
  881.9 4.1 multiply_reduce_fusion.2
  889.8 3.3 convolution_convert_fusion.2
  894.9 4.2 multiply_reduce_fusion.1
  903.1 4.4 fusion.30
  911.4 4.4 fusion.28
  919.7 3.3 convolution_convert_fusion
  923.0 8.5 fusion.55
  931.6 7.3 fusion.53
  941.1 3.7 broadcast_multiply_fusion.1
  953.4 25.2 reduce-scatter.17.cloned.1.call-done
  980.1 44.6 %reduce-scatter.15.cloned.1.call-done = f32[256,512]{1,0:T(8,128)} async-done(((f32[1024,512]{1,0:T(8,128)}), f32[256,512]{1,0:T(8,128)}) %reduce-scatter.15.cloned.1.call-update) | async-done | bytes 524304 | tf_op jit(solution)/shard_map/reduce_scatter | solution.py:204
  1025.8 45.0 %reduce-scatter.19.cloned.1.call-done = f32[256,512]{1,0:T(8,128)} async-done(((f32[1024,512]{1,0:T(8,128)}), f32[256,512]{1,0:T(8,128)}) %reduce-scatter.19.cloned.1.call-update) | async-done | bytes 524304 | tf_op jit(solution)/shard_map/reduce_scatter | solution.py:204
  1071.8 6.0 convolution_bitcast_fusion.3
  1077.8 6.0 convolution_bitcast_fusion.2
  1084.3 8.3 convert_bitcast_fusion.2
  1092.7 8.5 convert_bitcast_fusion.3
  1101.8 5.8 convert_bitcast_fusion.4
  1108.6 5.9 convert_bitcast_fusion.5
  1115.1 14.1 convert_bitcast_fusion
  1129.8 11.3 convert_bitcast_fusion.1
  1144.2 5.3 copy.151
  1158.6 5.4 copy.146
  1164.0 5.4 copy.143
  1175.2 36.4 %reduce-scatter.25.cloned.1.call-done = bf16[256,512]{1,0:T(8,128)(2,1)} async-done(((bf16[2048,512]{1,0:T(8,128)(2,1)}), bf16[256,512]{1,0:T(8,128)(2,1)}) %reduce-scatter.25.cloned.1.call-update) | async-done | bytes 262160 | tf_op jit(solution)/shard_map/reduce_scatter | solution.py:87
  1214.1 154.7 %all-reduce.21.cloned.1.call-done = (f32[256,2048]{1,0:T(8,128)}, f32[256,2048]{1,0:T(8,128)}, f32[256,2048]{1,0:T(8,128)}, f32[256,2048]{1,0:T(8,128)}) async-done(((f32[256,2048]{1,0:T(8,128)}, f32[256,2048]{1,0:T(8,128)}, f32[256,2048]{1,0:T(8,128)}, f32[256,2048]{1,0:T(8,128)}), (f32[256,2048]{1,0:T(8,128)}, f32[256,2048]{1,0:T(8,128)}, f32[256,2048]{1,0:T(8,128)}, ...) | async-done | bytes 8388624 | tf_op jit(solution)/shard_map/psum | solution.py:62
  1368.8 3.7 fusion.19
  1385.3 136.6 %reduce-scatter.35.cloned.1.call-done = bf16[256,2048]{0,1:T(8,128)(2,1)} async-done(((bf16[2048,2048]{0,1:T(8,128)(2,1)}), bf16[256,2048]{0,1:T(8,128)(2,1)}) %reduce-scatter.35.cloned.1.call-update) | async-done | bytes 1048592 | tf_op jit(solution)/shard_map/reduce_scatter | solution.py:90
  1521.9 152.5 %reduce-scatter.33.cloned.1.call-done = bf16[256,2048]{0,1:T(8,128)(2,1)} async-done(((bf16[2048,2048]{0,1:T(8,128)(2,1)}), bf16[256,2048]{0,1:T(8,128)(2,1)}) %reduce-scatter.33.cloned.1.call-update) | async-done | bytes 1048592 | tf_op jit(solution)/shard_map/reduce_scatter | solution.py:90
  1677.1 118.2 %reduce-scatter.23.cloned.1.call-done = bf16[3,256,512]{1,2,0:T(8,128)(2,1)} async-done(((bf16[3,2048,512]{1,2,0:T(8,128)(2,1)}), bf16[3,256,512]{1,2,0:T(8,128)(2,1)}) %reduce-scatter.23.cloned.1.call-update) | async-done | bytes 786448 | tf_op jit(solution)/shard_map/reduce_scatter | solution.py:79
  1795.2 121.2 %reduce-scatter.21.cloned.1.call-done = bf16[3,256,512]{1,2,0:T(8,128)(2,1)} async-done(((bf16[3,2048,512]{1,2,0:T(8,128)(2,1)}), bf16[3,256,512]{1,2,0:T(8,128)(2,1)}) %reduce-scatter.21.cloned.1.call-update) | async-done | bytes 786448 | tf_op jit(solution)/shard_map/reduce_scatter | solution.py:79
  1920.1 281.2 %reduce-scatter.31.cloned.1.call-done = bf16[2,256,2048]{1,2,0:T(8,128)(2,1)} async-done(((bf16[2,2048,2048]{1,2,0:T(8,128)(2,1)}), bf16[2,256,2048]{1,2,0:T(8,128)(2,1)}) %reduce-scatter.31.cloned.1.call-update) | async-done | bytes 2097168 | tf_op jit(solution)/shard_map/reduce_scatter | solution.py:82
  2201.4 285.4 %reduce-scatter.29.cloned.1.call-done = bf16[2,256,2048]{1,2,0:T(8,128)(2,1)} async-done(((bf16[2,2048,2048]{1,2,0:T(8,128)(2,1)}), bf16[2,256,2048]{1,2,0:T(8,128)(2,1)}) %reduce-scatter.29.cloned.1.call-update) | async-done | bytes 2097168 | tf_op jit(solution)/shard_map/reduce_scatter | solution.py:82
  2486.7 3.9 multiply_reduce_fusion
  2492.0 3.2 pad_maximum_fusion.1
  2495.2 39.1 %psum.98 = f32[]{:T(128)} all-reduce(f32[]{:T(128)S(6)} %add.301), channel_id=1, replica_groups=mesh['fsdp'=2,'ctx'=4,'tp'=4] {'fsdp','ctx','tp'}, use_global_device_ids=true, to_apply=%region_41.42 | all-reduce | flops 1 | bytes 8 | tf_op jit(solution)/shard_map/psum | solution.py:268
  2535.0 5.4 fusion.122
  2540.4 3.2 copy.154
  2543.6 12.4 fusion.118
  2556.0 5.5 copy.155
  2561.5 7.0 fusion.116
  2573.2 5.5 copy.158
  2583.5 5.5 copy.161
  2593.8 5.3 copy.164
  (397 shorter events, 166.6 us)
Async XLA Ops:
  7.2 105.3 %all-gather.11.cloned.1.call-start = ((), (), s32[]{:S(2)}) async-start(), calls=%async_computation.12 | async-start | bytes 7077888 | tf_op jit(solution)/shard_map/all_gather | solution.py:67
  9.6 4.2 copy-start.8
  9.7 144.5 %all-gather.21.cloned.1.call-start = ((), (), s32[]{:S(2)}) async-start(), calls=%async_computation.17 | async-start | bytes 1310720 | tf_op jit(solution)/shard_map/all_gather | solution.py:126
  14.2 118.6 %copy-start.73 = (f32[256]{0:T(256)}, f32[256]{0:T(256)S(1)}, u32[]{:S(2)}) copy-start(f32[256]{0:T(256)S(1)} %broadcast_multiply_fusion.13) | copy-start | bytes 3076
  14.2 103.0 %copy-start.75 = (f32[256]{0:T(256)}, f32[256]{0:T(256)S(1)}, u32[]{:S(2)}) copy-start(f32[256]{0:T(256)S(1)} %broadcast_multiply_fusion.11) | copy-start | bytes 3076
  14.9 102.3 %copy-start.96 = (f32[256]{0:T(256)}, f32[256]{0:T(256)S(1)}, u32[]{:S(2)}) copy-start(f32[256]{0:T(256)S(1)} %get-tuple-element.74) | copy-start | bytes 3076
  14.9 116.0 %copy-start.98 = (f32[256]{0:T(256)}, f32[256]{0:T(256)S(1)}, u32[]{:S(2)}) copy-start(f32[256]{0:T(256)S(1)} %get-tuple-element.73) | copy-start | bytes 3076
  14.9 102.2 %copy-start.88 = (f32[256]{0:T(256)}, f32[256]{0:T(256)S(1)}, u32[]{:S(2)}) copy-start(f32[256]{0:T(256)S(1)} %fusion.98) | copy-start | bytes 3076
  127.9 55.9 %all-gather.25.cloned.1.call-start = ((), (), s32[]{:S(2)}) async-start(), calls=%async_computation.31 | async-start | bytes 1310720 | tf_op jit(solution)/shard_map/all_gather | solution.py:127
  130.9 6.7 copy-start.90
  132.7 80.5 %all-gather.13.cloned.1.call-start = ((), (), s32[]{:S(2)}) async-start(), calls=%async_computation.13 | async-start | bytes 1310720 | tf_op jit(solution)/shard_map/all_gather | solution.py:126
  141.2 3.8 copy-start.51
  142.2 4.1 copy-start.103
  142.2 4.1 copy-start.106
  142.2 5.1 copy-start.101
  142.2 5.1 copy-start.105
  144.2 98.5 %all-gather.23.cloned.1.call-start = ((), (), s32[]{:S(2)}) async-start(), calls=%async_computation.30 | async-start | bytes 1310720 | tf_op jit(solution)/shard_map/all_gather | solution.py:127
  145.0 149.0 %all-gather.15.cloned.1.call-start = ((), (), s32[]{:S(2)}) async-start(), calls=%async_computation.14 | async-start | bytes 2359296 | tf_op jit(solution)/shard_map/all_gather | solution.py:71
  145.8 238.4 %all-reduce.25.cloned.1.call-start = ((), (), s32[]{:S(2)}) async-start(), calls=%async_computation.34 | async-start | bytes 8388608 | tf_op jit(solution)/shard_map/psum | solution.py:62
  185.1 65.4 %copy-start.41 = (bf16[1024,4,128]{2,1,0:T(4,128)(2,1)}, bf16[1024,4,128]{2,1,0:T(4,128)(2,1)S(1)}, u32[]{:S(2)}) copy-start(bf16[1024,4,128]{2,1,0:T(4,128)(2,1)S(1)} %reshape.480) | copy-start | bytes 3145732
  214.7 33.2 %copy-start.20 = (bf16[1024,512]{0,1:T(8,128)(2,1)}, bf16[1024,512]{0,1:T(8,128)(2,1)S(1)}, u32[]{:S(2)}) copy-start(bf16[1024,512]{0,1:T(8,128)(2,1)S(1)} %copy.185) | copy-start | bytes 3145732
  252.1 41.9 %copy-start.65 = (bf16[4,128,256]{2,1,0:T(8,128)(2,1)}, bf16[4,128,256]{2,1,0:T(8,128)(2,1)S(1)}, u32[]{:S(2)}) copy-start(bf16[4,128,256]{2,1,0:T(8,128)(2,1)S(1)} %fusion.47) | copy-start | bytes 786436
  253.3 44.5 %copy-start.63 = (bf16[4,128,256]{2,1,0:T(8,128)(2,1)}, bf16[4,128,256]{2,1,0:T(8,128)(2,1)S(1)}, u32[]{:S(2)}) copy-start(bf16[4,128,256]{2,1,0:T(8,128)(2,1)S(1)} %fusion.48) | copy-start | bytes 786436
  294.0 3.8 copy-start.27
  299.9 315.0 %all-gather.17.cloned.1.call-start = ((), (), s32[]{:S(2)}) async-start(), calls=%async_computation.15 | async-start | bytes 18874368 | tf_op jit(solution)/shard_map/all_gather | solution.py:68
  303.9 437.2 %all-gather.19.cloned.1.call-start = ((), (), s32[]{:S(2)}) async-start(), calls=%async_computation.16 | async-start | bytes 9437184 | tf_op jit(solution)/shard_map/all_gather | solution.py:72
  306.8 562.1 %all-reduce.23.cloned.1.call-start = ((), (), s32[]{:S(2)}) async-start(), calls=%async_computation.33 | async-start | bytes 8388608 | tf_op jit(solution)/shard_map/psum | solution.py:62
  389.5 238.6 %copy-start.77 = (f32[256]{0:T(256)}, f32[256]{0:T(256)S(1)}, u32[]{:S(2)}) copy-start(f32[256]{0:T(256)S(1)} %fusion.97) | copy-start | bytes 3076
  615.0 13.2 copy-start.7
  741.0 10.6 copy-start.18
  741.0 10.6 copy-start.29
  741.0 10.6 copy-start.108
  784.9 165.8 %reduce-scatter.13.cloned.1.call-start = ((), (), s32[]{:S(2)}) async-start(), calls=%async_computation.18 | async-start | bytes 2621440 | tf_op jit(solution)/shard_map/reduce_scatter | solution.py:201
  881.9 4.1 copy-start.6
  889.0 89.6 %reduce-scatter.17.cloned.1.call-start = ((), (), s32[]{:S(2)}) async-start(), calls=%async_computation.20 | async-start | bytes 2621440 | tf_op jit(solution)/shard_map/reduce_scatter | solution.py:201
  894.9 4.2 copy-start.4
  902.2 122.5 %reduce-scatter.15.cloned.1.call-start = ((), (), s32[]{:S(2)}) async-start(), calls=%async_computation.19 | async-start | bytes 2621440 | tf_op jit(solution)/shard_map/reduce_scatter | solution.py:204
  910.4 160.3 %reduce-scatter.19.cloned.1.call-start = ((), (), s32[]{:S(2)}) async-start(), calls=%async_computation.21 | async-start | bytes 2621440 | tf_op jit(solution)/shard_map/reduce_scatter | solution.py:204
  918.7 256.4 %reduce-scatter.27.cloned.1.call-start = ((), (), s32[]{:S(2)}) async-start(), calls=%async_computation.25 | async-start | bytes 2359296 | tf_op jit(solution)/shard_map/reduce_scatter | solution.py:87
  923.0 288.6 %reduce-scatter.25.cloned.1.call-start = ((), (), s32[]{:S(2)}) async-start(), calls=%async_computation.24 | async-start | bytes 2359296 | tf_op jit(solution)/shard_map/reduce_scatter | solution.py:87
  923.0 8.6 copy-start.19
  931.6 7.3 copy-start.39
  931.6 7.3 copy-start.64
  944.8 424.0 %all-reduce.21.cloned.1.call-start = ((), (), s32[]{:S(2)}) async-start(), calls=%async_computation.32 | async-start | bytes 16777216 | tf_op jit(solution)/shard_map/psum | solution.py:62
  951.3 27.3 %copy-start.60 = (f32[256,128]{0,1:T(8,128)S(1)}, f32[256,128]{0,1:T(8,128)}, u32[]{:S(2)}) copy-start(f32[256,128]{0,1:T(8,128)} %get-tuple-element.156) | copy-start | bytes 393220
  979.8 92.1 %copy-start.70 = (bf16[1,256,512]{2,1,0:T(8,128)(2,1)S(1)}, bf16[1,256,512]{2,1,0:T(8,128)(2,1)}, u32[]{:S(2)}) copy-start(bf16[1,256,512]{2,1,0:T(8,128)(2,1)} %copy.130) | copy-start | bytes 786436
  1083.9 438.0 %reduce-scatter.35.cloned.1.call-start = ((), (), s32[]{:S(2)}) async-start(), calls=%async_computation.29 | async-start | bytes 9437184 | tf_op jit(solution)/shard_map/reduce_scatter | solution.py:90
  1092.6 581.7 %reduce-scatter.33.cloned.1.call-start = ((), (), s32[]{:S(2)}) async-start(), calls=%async_computation.28 | async-start | bytes 9437184 | tf_op jit(solution)/shard_map/reduce_scatter | solution.py:90
  1101.2 694.0 %reduce-scatter.23.cloned.1.call-start = ((), (), s32[]{:S(2)}) async-start(), calls=%async_computation.23 | async-start | bytes 7077888 | tf_op jit(solution)/shard_map/reduce_scatter | solution.py:79
  1107.7 808.8 %reduce-scatter.21.cloned.1.call-start = ((), (), s32[]{:S(2)}) async-start(), calls=%async_computation.22 | async-start | bytes 7077888 | tf_op jit(solution)/shard_map/reduce_scatter | solution.py:79
  1114.5 1086.9 %reduce-scatter.31.cloned.1.call-start = ((), (), s32[]{:S(2)}) async-start(), calls=%async_computation.27 | async-start | bytes 18874368 | tf_op jit(solution)/shard_map/reduce_scatter | solution.py:82
  1129.2 1357.5 %reduce-scatter.29.cloned.1.call-start = ((), (), s32[]{:S(2)}) async-start(), calls=%async_computation.26 | async-start | bytes 18874368 | tf_op jit(solution)/shard_map/reduce_scatter | solution.py:82
  1368.8 3.7 copy-start.97
  1368.8 3.8 copy-start.9
  1368.8 4.1 copy-start.16
  1368.8 4.7 copy-start.17
  1378.2 3.9 copy-start.55
  2491.9 43.0 %copy-start.34 = (f32[3,256,512]{1,2,0:T(8,128)S(1)}, f32[3,256,512]{1,2,0:T(8,128)}, u32[]{:S(2)}) copy-start(f32[3,256,512]{1,2,0:T(8,128)} %copy.149) | copy-start | bytes 4718596
  2492.0 43.0 %copy-start.35 = (f32[3,256,512]{1,2,0:T(8,128)S(1)}, f32[3,256,512]{1,2,0:T(8,128)}, u32[]{:S(2)}) copy-start(f32[3,256,512]{1,2,0:T(8,128)} %copy.145) | copy-start | bytes 4718596
  2556.0 5.5 copy-start.22
  2556.0 5.5 copy-start.37
  2573.2 5.5 copy-start.25
  2583.5 5.5 copy-start.24
  2599.2 4.2 copy-start.23
  (68 other events, 128.7 us)
Sparse Core Ops, SparseCore 0:
  10.8 101.7 all-gather.10
  128.0 26.1 all-gather.20
  156.3 27.4 all-gather.24
  185.8 27.4 all-gather.12
  215.2 27.4 all-gather.22
  245.2 48.7 all-gather.14
  300.1 84.1 all-reduce.24
  387.2 227.7 all-gather.16
  617.9 123.0 all-gather.18
  785.1 83.8 all-reduce.22
  889.1 43.9 reduce-scatter.12
  935.4 43.1 reduce-scatter.16
  981.5 43.1 reduce-scatter.14
  1027.5 43.1 reduce-scatter.18
  1074.1 67.0 reduce-scatter.26
  1144.6 66.9 reduce-scatter.24
  1215.8 152.9 all-reduce.20
  1372.3 149.5 reduce-scatter.34
  1525.9 148.4 reduce-scatter.32
  1677.8 117.3 reduce-scatter.22
  1798.8 117.5 reduce-scatter.20
  1920.2 281.0 reduce-scatter.30
  2205.6 281.0 reduce-scatter.28
where the time goes:
time: 2630 us; the launch traced here: 2620 us
  waiting for transfers between devices  2120 us (81%)
  matrix products  204 us (8%)
  local copies, waits for them, and re-layouts  129 us (5%)
  other arithmetic  101 us (4%)
  blocking collectives  39.1 us (1%)
    reduce_scatter x2, waiting for transfers between devices, reduce_grads(): lax.psum_scatter(proj_grad.astype(jnp.bfloat16), ('fsdp', 'ctx'), scatter...  567 us
    psum x3, waiting for transfers between devices, tensor_sum(): return lax.psum(partial_sum, 'tp')  315 us
    reduce_scatter x2, waiting for transfers between devices, reduce_grads(): lax.psum_scatter(down_grad.astype(jnp.bfloat16), ('fsdp', 'ctx'), scatter...  289 us
    reduce_scatter x2, waiting for transfers between devices, reduce_grads(): lax.psum_scatter(att_grad.astype(jnp.bfloat16), ('fsdp', 'ctx'), scatter_...  239 us
    all_gather x1, waiting for transfers between devices, gather_weights(): lax.all_gather(ff_proj.astype(jnp.bfloat16), ('fsdp', 'ctx'), axis=1, til...  225 us
    all_gather x1, waiting for transfers between devices, gather_weights(): lax.all_gather(ff_out.astype(jnp.bfloat16), ('fsdp', 'ctx'), axis=0, tile...  107 us
    unnamed x242, local copies, waits for them, and re-layouts  102 us
    all_gather x1, waiting for transfers between devices, gather_weights(): lax.all_gather(att_proj.astype(jnp.bfloat16), ('fsdp', 'ctx'), axis=1, ti...  97.6 us
  transfers between devices with their start and end apart: 23, of which 21 were waited for; matrix products, arithmetic and copies ran while one was open for 10% of the time, Pallas kernels for 0%

commit v1 on v0

--- a/solution.py
+++ b/solution.py
@@ -15,6 +15,12 @@
 NEG_FILL = -1e30
 
 
+def add_all(block, axis):
+    blocks = lax.all_gather(block, axis, axis=0, tiled=False)
+    total = blocks.sum(axis=0)
+    return total
+
+
 def layer_norm(values):
     centre = values - jnp.mean(values, axis=-1, keepdims=True)
     spread = jnp.mean(centre * centre, axis=-1, keepdims=True)
@@ -59,7 +65,7 @@
 
 
 def tensor_sum(partial_sum):
-    return lax.psum(partial_sum, "tp")
+    return add_all(partial_sum, "tp")
 
 
 def gather_weights(att_proj, attn_out, ff_proj, ff_out):

time: 2630 us -> 2750 us (1.046)
  waiting for transfers between devices: 2120 us -> 2190 us
  other arithmetic: 101 us -> 161 us
    all_gather x0 -> x8, waiting for transfers between devices: none -> 328 us  [add_all(): blocks = lax.all_gather(block, axis, axis=0, tiled=False)]
    psum x3 -> x0, waiting for transfers between devices: 315 us -> none  [tensor_sum(): return lax.psum(partial_sum, 'tp')]
    reduce_scatter x2, waiting for transfers between devices: 36.4 us -> 135 us  [reduce_grads(): lax.psum_scatter(out_grad.astype(jnp.bfloat16), ('fsdp', 'ctx'), scatter_...]
    reduce_scatter x2, waiting for transfers between devices: 289 us -> 235 us  [reduce_grads(): lax.psum_scatter(down_grad.astype(jnp.bfloat16), ('fsdp', 'ctx'), scatter...]
    reduce_sum x0 -> x8, other arithmetic: none -> 45.9 us  [add_all(): total = blocks.sum(axis=0)]
    unnamed x242 -> x248, local copies, waits for them, and re-layouts: 102 us -> 96.1 us
  transfers between devices with their start and end apart: 23 -> 28, of which waited for: 21 -> 27; matrix products, arithmetic and copies ran while one was open for 10% -> 12% of each run, Pallas kernels for 0% -> 0%
where the time goes in v1:
time: 2750 us
  waiting for transfers between devices  2190 us (80%)
  matrix products  206 us (7%)
  other arithmetic  161 us (6%)
  local copies, waits for them, and re-layouts  123 us (4%)
  blocking collectives  39.1 us (1%)
    reduce_scatter x2, waiting for transfers between devices, reduce_grads(): lax.psum_scatter(proj_grad.astype(jnp.bfloat16), ('fsdp', 'ctx'), scatter...  566 us
    all_gather x8, waiting for transfers between devices, add_all(): blocks = lax.all_gather(block, axis, axis=0, tiled=False)  328 us
    reduce_scatter x2, waiting for transfers between devices, reduce_grads(): lax.psum_scatter(att_grad.astype(jnp.bfloat16), ('fsdp', 'ctx'), scatter_...  239 us
    reduce_scatter x2, waiting for transfers between devices, reduce_grads(): lax.psum_scatter(down_grad.astype(jnp.bfloat16), ('fsdp', 'ctx'), scatter...  235 us
    all_gather x1, waiting for transfers between devices, gather_weights(): lax.all_gather(ff_proj.astype(jnp.bfloat16), ('fsdp', 'ctx'), axis=1, til...  219 us
    reduce_scatter x2, waiting for transfers between devices, reduce_grads(): lax.psum_scatter(out_grad.astype(jnp.bfloat16), ('fsdp', 'ctx'), scatter_...  135 us
    all_gather x1, waiting for transfers between devices, gather_weights(): lax.all_gather(ff_out.astype(jnp.bfloat16), ('fsdp', 'ctx'), axis=0, tile...  115 us
    all_gather x1, waiting for transfers between devices, gather_weights(): lax.all_gather(att_proj.astype(jnp.bfloat16), ('fsdp', 'ctx'), axis=1, ti...  97.6 us
  transfers between devices with their start and end apart: 28, of which 27 were waited for; matrix products, arithmetic and copies ran while one was open for 12% of the time, Pallas kernels for 0%

profile of v1, /device:TPU:0, one launch (start us, length us, event | category | flops | bytes accessed | tf_op | source)
XLA Modules:
  0.0 2746.3 jit_solution(248620134804033783)
XLA Ops:
  14.9 97.6 %all-gather.27.cloned.1.call-done = bf16[3,2048,512]{2,1,0:T(8,128)(2,1)} async-done(((bf16[3,256,512]{2,1,0:T(8,128)(2,1)}), bf16[3,2048,512]{2,1,0:T(8,128)(2,1)}) %all-gather.27.cloned.1.call-update) | async-done | bytes 6291472 | tf_op jit(solution)/shard_map/all_gather | solution.py:73
  145.0 10.2 all-gather.29.cloned.1.call-done
  156.6 28.1 %all-gather.39.cloned.1.call-done = bf16[1,1024,512]{2,1,0:T(8,128)(2,1)} async-done(((bf16[1,256,512]{2,1,0:T(8,128)(2,1)}), bf16[1,1024,512]{2,1,0:T(8,128)(2,1)}) %all-gather.39.cloned.1.call-update) | async-done | bytes 1048592 | tf_op jit(solution)/shard_map/all_gather | solution.py:133
  190.5 45.6 %all-gather.31.cloned.1.call-done = bf16[2048,512]{1,0:T(8,128)(2,1)} async-done(((bf16[256,512]{1,0:T(8,128)(2,1)}), bf16[2048,512]{1,0:T(8,128)(2,1)}) %all-gather.31.cloned.1.call-update) | async-done | bytes 2097168 | tf_op jit(solution)/shard_map/all_gather | solution.py:77
  241.5 23.1 all-gather.37.cloned.1.call-done
  266.1 28.0 %all-gather.45.cloned.1.call-done = bf16[1,1024,512]{2,1,0:T(8,128)(2,1)} async-done(((bf16[1,256,512]{2,1,0:T(8,128)(2,1)}), bf16[1,1024,512]{2,1,0:T(8,128)(2,1)}) %all-gather.45.cloned.1.call-update) | async-done | bytes 1048592 | tf_op jit(solution)/shard_map/all_gather | solution.py:133
  311.3 42.6 %all-gather.41.cloned.1.call-done = f32[1024,2048]{1,0:T(8,128)} async-done(((f32[256,2048]{1,0:T(8,128)}), f32[1024,2048]{1,0:T(8,128)}) %all-gather.41.cloned.1.call-update) | async-done | bytes 8388624 | tf_op jit(solution)/shard_map/all_gather | solution.py:19
  354.0 5.7 reduce_sum.358
  359.7 54.7 %all-gather.47.cloned.1.call-done = f32[1024,2048]{1,0:T(8,128)} async-done(((f32[256,2048]{1,0:T(8,128)}), f32[1024,2048]{1,0:T(8,128)}) %all-gather.47.cloned.1.call-update) | async-done | bytes 8388624 | tf_op jit(solution)/shard_map/all_gather | solution.py:19
  414.4 5.7 reduce_sum.368
  420.2 5.2 fusion.146
  425.7 219.1 %all-gather.33.cloned.1.call-done = bf16[2,2048,2048]{2,1,0:T(8,128)(2,1)} async-done(((bf16[2,256,2048]{2,1,0:T(8,128)(2,1)}), bf16[2,2048,2048]{2,1,0:T(8,128)(2,1)}) %all-gather.33.cloned.1.call-update) | async-done | bytes 16777232 | tf_op jit(solution)/shard_map/all_gather | solution.py:74
  644.8 10.3 convolution_bitcast_fusion.1
  655.1 115.4 %all-gather.35.cloned.1.call-done = bf16[2048,2048]{1,0:T(8,128)(2,1)} async-done(((bf16[256,2048]{1,0:T(8,128)(2,1)}), bf16[2048,2048]{1,0:T(8,128)(2,1)}) %all-gather.35.cloned.1.call-update) | async-done | bytes 8388624 | tf_op jit(solution)/shard_map/all_gather | solution.py:78
  770.5 10.4 multiply_bitcast_fusion.3
  780.9 13.5 convolution_bitcast_fusion.5
  797.8 11.0 convolution_bitcast_fusion
  808.9 5.6 multiply_bitcast_fusion.1
  814.4 13.5 convolution_bitcast_fusion.4
  829.2 21.9 all-gather.51.cloned.1.call-done
  851.1 5.7 reduce_sum.374
  859.4 51.4 %all-gather.55.cloned.1.call-done = f32[1024,2048]{1,0:T(8,128)} async-done(((f32[256,2048]{1,0:T(8,128)}), f32[1024,2048]{1,0:T(8,128)}) %all-gather.55.cloned.1.call-update) | async-done | bytes 8388624 | tf_op jit(solution)/shard_map/all_gather | solution.py:19
  910.8 5.9 reduce_sum.383
  965.8 8.3 fusion.65
  982.7 43.1 %reduce-scatter.19.cloned.1.call-done = f32[256,512]{1,0:T(8,128)} async-done(((f32[1024,512]{1,0:T(8,128)}), f32[256,512]{1,0:T(8,128)}) %reduce-scatter.19.cloned.1.call-update) | async-done | bytes 524304 | tf_op jit(solution)/shard_map/reduce_scatter | solution.py:210
  1026.8 6.1 convolution_bitcast_fusion.2
  1036.7 34.4 %reduce-scatter.13.cloned.1.call-done = f32[256,512]{0,1:T(8,128)} async-done(((f32[1024,512]{0,1:T(8,128)}), f32[256,512]{0,1:T(8,128)}) %reduce-scatter.13.cloned.1.call-update) | async-done | bytes 524304 | tf_op jit(solution)/shard_map/reduce_scatter | solution.py:207
  1072.6 44.6 %reduce-scatter.15.cloned.1.call-done = f32[256,512]{1,0:T(8,128)} async-done(((f32[1024,512]{1,0:T(8,128)}), f32[256,512]{1,0:T(8,128)}) %reduce-scatter.15.cloned.1.call-update) | async-done | bytes 524304 | tf_op jit(solution)/shard_map/reduce_scatter | solution.py:210
  1118.2 5.9 convolution_bitcast_fusion.3
  1124.2 10.6 fusion.63
  1135.1 8.4 convert_bitcast_fusion.2
  1143.5 8.3 convert_bitcast_fusion.3
  1152.9 5.8 convert_bitcast_fusion.4
  1159.7 5.8 convert_bitcast_fusion.5
  1166.0 10.2 all-gather.49.cloned.1.call-done
  1176.2 5.7 reduce_sum.372
  1181.9 54.6 %all-gather.57.cloned.1.call-done = f32[1024,2048]{1,0:T(8,128)} async-done(((f32[256,2048]{1,0:T(8,128)}), f32[1024,2048]{1,0:T(8,128)}) %all-gather.57.cloned.1.call-update) | async-done | bytes 8388624 | tf_op jit(solution)/shard_map/all_gather | solution.py:19
  1236.5 5.7 reduce_sum.387
  1242.2 54.7 %all-gather.53.cloned.1.call-done = f32[1024,2048]{1,0:T(8,128)} async-done(((f32[256,2048]{1,0:T(8,128)}), f32[1024,2048]{1,0:T(8,128)}) %all-gather.53.cloned.1.call-update) | async-done | bytes 8388624 | tf_op jit(solution)/shard_map/all_gather | solution.py:19
  1297.0 5.7 reduce_sum.378
  1318.8 37.9 %all-gather.43.cloned.1.call-done = f32[1024,2048]{1,0:T(8,128)} async-done(((f32[256,2048]{1,0:T(8,128)}), f32[1024,2048]{1,0:T(8,128)}) %all-gather.43.cloned.1.call-update) | async-done | bytes 8388624 | tf_op jit(solution)/shard_map/all_gather | solution.py:19
  1356.7 5.7 reduce_sum.362
  1362.4 6.1 fusion.26
  1370.9 14.0 convert_bitcast_fusion
  1385.0 11.4 convert_bitcast_fusion.1
  1399.5 5.7 copy.151
  1411.7 5.4 copy.146
  1417.1 5.6 copy.143
  1427.4 82.4 %reduce-scatter.35.cloned.1.call-done = bf16[256,2048]{0,1:T(8,128)(2,1)} async-done(((bf16[2048,2048]{0,1:T(8,128)(2,1)}), bf16[256,2048]{0,1:T(8,128)(2,1)}) %reduce-scatter.35.cloned.1.call-update) | async-done | bytes 1048592 | tf_op jit(solution)/shard_map/reduce_scatter | solution.py:96
  1509.8 152.6 %reduce-scatter.33.cloned.1.call-done = bf16[256,2048]{0,1:T(8,128)(2,1)} async-done(((bf16[2048,2048]{0,1:T(8,128)(2,1)}), bf16[256,2048]{0,1:T(8,128)(2,1)}) %reduce-scatter.33.cloned.1.call-update) | async-done | bytes 1048592 | tf_op jit(solution)/shard_map/reduce_scatter | solution.py:96
  1665.0 118.3 %reduce-scatter.23.cloned.1.call-done = bf16[3,256,512]{1,2,0:T(8,128)(2,1)} async-done(((bf16[3,2048,512]{1,2,0:T(8,128)(2,1)}), bf16[3,256,512]{1,2,0:T(8,128)(2,1)}) %reduce-scatter.23.cloned.1.call-update) | async-done | bytes 786448 | tf_op jit(solution)/shard_map/reduce_scatter | solution.py:85
  1783.3 121.0 %reduce-scatter.21.cloned.1.call-done = bf16[3,256,512]{1,2,0:T(8,128)(2,1)} async-done(((bf16[3,2048,512]{1,2,0:T(8,128)(2,1)}), bf16[3,256,512]{1,2,0:T(8,128)(2,1)}) %reduce-scatter.21.cloned.1.call-update) | async-done | bytes 786448 | tf_op jit(solution)/shard_map/reduce_scatter | solution.py:85
  1910.8 64.7 %reduce-scatter.27.cloned.1.call-done = bf16[256,512]{1,0:T(8,128)(2,1)} async-done(((bf16[2048,512]{1,0:T(8,128)(2,1)}), bf16[256,512]{1,0:T(8,128)(2,1)}) %reduce-scatter.27.cloned.1.call-update) | async-done | bytes 262160 | tf_op jit(solution)/shard_map/reduce_scatter | solution.py:93
  1975.4 70.3 %reduce-scatter.25.cloned.1.call-done = bf16[256,512]{1,0:T(8,128)(2,1)} async-done(((bf16[2048,512]{1,0:T(8,128)(2,1)}), bf16[256,512]{1,0:T(8,128)(2,1)}) %reduce-scatter.25.cloned.1.call-update) | async-done | bytes 262160 | tf_op jit(solution)/shard_map/reduce_scatter | solution.py:93
  2049.5 280.9 %reduce-scatter.31.cloned.1.call-done = bf16[2,256,2048]{1,2,0:T(8,128)(2,1)} async-done(((bf16[2,2048,2048]{1,2,0:T(8,128)(2,1)}), bf16[2,256,2048]{1,2,0:T(8,128)(2,1)}) %reduce-scatter.31.cloned.1.call-update) | async-done | bytes 2097168 | tf_op jit(solution)/shard_map/reduce_scatter | solution.py:88
  2330.4 285.3 %reduce-scatter.29.cloned.1.call-done = bf16[2,256,2048]{1,2,0:T(8,128)(2,1)} async-done(((bf16[2,2048,2048]{1,2,0:T(8,128)(2,1)}), bf16[2,256,2048]{1,2,0:T(8,128)(2,1)}) %reduce-scatter.29.cloned.1.call-update) | async-done | bytes 2097168 | tf_op jit(solution)/shard_map/reduce_scatter | solution.py:88
  2624.1 39.1 %psum.34 = f32[]{:T(128)} all-reduce(f32[]{:T(128)S(6)} %add.311), channel_id=1, replica_groups=mesh['fsdp'=2,'ctx'=4,'tp'=4] {'fsdp','ctx','tp'}, use_global_device_ids=true, to_apply=%region_41.42 | all-reduce | flops 1 | bytes 8 | tf_op jit(solution)/shard_map/psum | solution.py:274
  2663.9 5.4 fusion.140
  2672.6 12.4 fusion.136
  2685.0 5.5 copy.155
  2690.5 7.0 fusion.134
  2702.1 5.5 copy.158
  2712.5 5.5 copy.161
  2722.8 5.3 copy.164
  (425 shorter events, 224.7 us)
Async XLA Ops:
  7.2 105.3 %all-gather.27.cloned.1.call-start = ((), (), s32[]{:S(2)}) async-start(), calls=%async_computation.12 | async-start | bytes 7077888 | tf_op jit(solution)/shard_map/all_gather | solution.py:73
  9.7 145.5 %all-gather.29.cloned.1.call-start = ((), (), s32[]{:S(2)}) async-start(), calls=%async_computation.13 | async-start | bytes 1310720 | tf_op jit(solution)/shard_map/all_gather | solution.py:132
  13.6 109.2 %copy-start.50 = (f32[256,128]{0,1:T(8,128)}, f32[256,128]{0,1:T(8,128)S(1)}, u32[]{:S(2)}) copy-start(f32[256,128]{0,1:T(8,128)S(1)} %get-tuple-element.151) | copy-start | bytes 393220
  14.2 103.0 %copy-start.78 = (f32[256]{0:T(256)}, f32[256]{0:T(256)S(1)}, u32[]{:S(2)}) copy-start(f32[256]{0:T(256)S(1)} %broadcast_multiply_fusion.13) | copy-start | bytes 3076
  14.2 118.9 %copy-start.80 = (f32[256]{0:T(256)}, f32[256]{0:T(256)S(1)}, u32[]{:S(2)}) copy-start(f32[256]{0:T(256)S(1)} %broadcast_multiply_fusion.11) | copy-start | bytes 3076
  14.9 102.3 %copy-start.93 = (f32[256]{0:T(256)}, f32[256]{0:T(256)S(1)}, u32[]{:S(2)}) copy-start(f32[256]{0:T(256)S(1)} %get-tuple-element.73) | copy-start | bytes 3076
  14.9 118.2 %copy-start.91 = (f32[256]{0:T(256)}, f32[256]{0:T(256)S(1)}, u32[]{:S(2)}) copy-start(f32[256]{0:T(256)S(1)} %get-tuple-element.74) | copy-start | bytes 3076
  14.9 102.3 %copy-start.87 = (f32[256]{0:T(256)}, f32[256]{0:T(256)S(1)}, u32[]{:S(2)}) copy-start(f32[256]{0:T(256)S(1)} %fusion.116) | copy-start | bytes 3076
  124.7 6.0 copy-start.44
  128.9 55.9 %all-gather.39.cloned.1.call-start = ((), (), s32[]{:S(2)}) async-start(), calls=%async_computation.30 | async-start | bytes 1310720 | tf_op jit(solution)/shard_map/all_gather | solution.py:133
  130.7 105.4 %all-gather.31.cloned.1.call-start = ((), (), s32[]{:S(2)}) async-start(), calls=%async_computation.14 | async-start | bytes 2359296 | tf_op jit(solution)/shard_map/all_gather | solution.py:77
  131.6 133.0 %all-gather.37.cloned.1.call-start = ((), (), s32[]{:S(2)}) async-start(), calls=%async_computation.17 | async-start | bytes 1310720 | tf_op jit(solution)/shard_map/all_gather | solution.py:132
  142.6 151.4 %all-gather.45.cloned.1.call-start = ((), (), s32[]{:S(2)}) async-start(), calls=%async_computation.33 | async-start | bytes 1310720 | tf_op jit(solution)/shard_map/all_gather | solution.py:133
  144.5 41.7 %copy-start.55 = (pred[256,1024]{1,0:T(8,128)(4,1)S(1)}, pred[256,1024]{1,0:T(8,128)(4,1)}, u32[]{:S(2)}) copy-start(pred[256,1024]{1,0:T(8,128)(4,1)} %compare_and_fusion.1) | copy-start | bytes 786436
  144.5 209.5 %all-gather.41.cloned.1.call-start = ((), (), s32[]{:S(2)}) async-start(), calls=%async_computation.31 | async-start | bytes 10485760 | tf_op jit(solution)/shard_map/all_gather | solution.py:19
  190.5 49.3 %copy-start.56 = (bf16[4,128,256]{2,1,0:T(8,128)(2,1)}, bf16[4,128,256]{2,1,0:T(8,128)(2,1)S(1)}, u32[]{:S(2)}) copy-start(bf16[4,128,256]{2,1,0:T(8,128)(2,1)S(1)} %fusion.60) | copy-start | bytes 786436
  239.8 174.6 %all-gather.47.cloned.1.call-start = ((), (), s32[]{:S(2)}) async-start(), calls=%async_computation.34 | async-start | bytes 10485760 | tf_op jit(solution)/shard_map/all_gather | solution.py:19
  266.1 31.8 %copy-start.16 = (bf16[1024,512]{0,1:T(8,128)(2,1)}, bf16[1024,512]{0,1:T(8,128)(2,1)S(1)}, u32[]{:S(2)}) copy-start(bf16[1024,512]{0,1:T(8,128)(2,1)S(1)} %copy.186) | copy-start | bytes 3145732
  304.0 340.8 %all-gather.33.cloned.1.call-start = ((), (), s32[]{:S(2)}) async-start(), calls=%async_computation.15 | async-start | bytes 18874368 | tf_op jit(solution)/shard_map/all_gather | solution.py:74
  308.4 462.1 %all-gather.35.cloned.1.call-start = ((), (), s32[]{:S(2)}) async-start(), calls=%async_computation.16 | async-start | bytes 9437184 | tf_op jit(solution)/shard_map/all_gather | solution.py:78
  311.1 540.0 %all-gather.51.cloned.1.call-start = ((), (), s32[]{:S(2)}) async-start(), calls=%async_computation.36 | async-start | bytes 10485760 | tf_op jit(solution)/shard_map/all_gather | solution.py:19
  425.7 229.4 %copy-start.84 = (f32[256]{0:T(256)}, f32[256]{0:T(256)S(1)}, u32[]{:S(2)}) copy-start(f32[256]{0:T(256)S(1)} %multiply_reduce_fusion.7) | copy-start | bytes 3076
  425.7 229.4 %copy-start.72 = (f32[256]{0:T(256)}, f32[256]{0:T(256)S(1)}, u32[]{:S(2)}) copy-start(f32[256]{0:T(256)S(1)} %fusion.117) | copy-start | bytes 3076
  794.4 116.4 %all-gather.55.cloned.1.call-start = ((), (), s32[]{:S(2)}) async-start(), calls=%async_computation.38 | async-start | bytes 10485760 | tf_op jit(solution)/shard_map/all_gather | solution.py:19
  795.1 13.7 slice-start
  797.8 11.0 copy-start.75
  797.8 11.0 copy-start.42
  797.8 11.0 slice-start.1
  808.9 5.6 copy-start.15
  828.0 152.5 %reduce-scatter.17.cloned.1.call-start = ((), (), s32[]{:S(2)}) async-start(), calls=%async_computation.20 | async-start | bytes 2621440 | tf_op jit(solution)/shard_map/reduce_scatter | solution.py:207
  920.2 5.1 copy-start.25
  920.2 5.1 copy-start.43
  935.7 90.0 %reduce-scatter.19.cloned.1.call-start = ((), (), s32[]{:S(2)}) async-start(), calls=%async_computation.21 | async-start | bytes 2621440 | tf_op jit(solution)/shard_map/reduce_scatter | solution.py:210
  943.2 127.9 %reduce-scatter.13.cloned.1.call-start = ((), (), s32[]{:S(2)}) async-start(), calls=%async_computation.18 | async-start | bytes 2621440 | tf_op jit(solution)/shard_map/reduce_scatter | solution.py:207
  957.5 159.6 %reduce-scatter.15.cloned.1.call-start = ((), (), s32[]{:S(2)}) async-start(), calls=%async_computation.19 | async-start | bytes 2621440 | tf_op jit(solution)/shard_map/reduce_scatter | solution.py:210
  965.8 210.4 %all-gather.49.cloned.1.call-start = ((), (), s32[]{:S(2)}) async-start(), calls=%async_computation.35 | async-start | bytes 10485760 | tf_op jit(solution)/shard_map/all_gather | solution.py:19
  974.2 262.3 %all-gather.57.cloned.1.call-start = ((), (), s32[]{:S(2)}) async-start(), calls=%async_computation.39 | async-start | bytes 10485760 | tf_op jit(solution)/shard_map/all_gather | solution.py:19
  1033.0 264.0 %all-gather.53.cloned.1.call-start = ((), (), s32[]{:S(2)}) async-start(), calls=%async_computation.37 | async-start | bytes 10485760 | tf_op jit(solution)/shard_map/all_gather | solution.py:19
  1036.4 34.7 %copy-start.53 = (f32[256,128]{0,1:T(8,128)S(1)}, f32[256,128]{0,1:T(8,128)}, u32[]{:S(2)}) copy-start(f32[256,128]{0,1:T(8,128)} %get-tuple-element.150) | copy-start | bytes 393220
  1036.4 35.9 %copy-start.51 = (f32[256,128]{0,1:T(8,128)S(1)}, f32[256,128]{0,1:T(8,128)}, u32[]{:S(2)}) copy-start(f32[256,128]{0,1:T(8,128)} %copy-done.50) | copy-start | bytes 393220
  1072.6 51.6 %copy-start.69 = (bf16[1,256,512]{2,1,0:T(8,128)(2,1)}, bf16[1,256,512]{2,1,0:T(8,128)(2,1)S(1)}, u32[]{:S(2)}) copy-start(bf16[1,256,512]{2,1,0:T(8,128)(2,1)S(1)} %copy.179) | copy-start | bytes 786436
  1124.2 232.5 %all-gather.43.cloned.1.call-start = ((), (), s32[]{:S(2)}) async-start(), calls=%async_computation.32 | async-start | bytes 10485760 | tf_op jit(solution)/shard_map/all_gather | solution.py:19
  1134.9 374.9 %reduce-scatter.35.cloned.1.call-start = ((), (), s32[]{:S(2)}) async-start(), calls=%async_computation.29 | async-start | bytes 9437184 | tf_op jit(solution)/shard_map/reduce_scatter | solution.py:96
  1143.5 518.8 %reduce-scatter.33.cloned.1.call-start = ((), (), s32[]{:S(2)}) async-start(), calls=%async_computation.28 | async-start | bytes 9437184 | tf_op jit(solution)/shard_map/reduce_scatter | solution.py:96
  1151.9 631.4 %reduce-scatter.23.cloned.1.call-start = ((), (), s32[]{:S(2)}) async-start(), calls=%async_computation.23 | async-start | bytes 7077888 | tf_op jit(solution)/shard_map/reduce_scatter | solution.py:85
  1158.8 745.6 %reduce-scatter.21.cloned.1.call-start = ((), (), s32[]{:S(2)}) async-start(), calls=%async_computation.22 | async-start | bytes 7077888 | tf_op jit(solution)/shard_map/reduce_scatter | solution.py:85
  1165.6 809.9 %reduce-scatter.27.cloned.1.call-start = ((), (), s32[]{:S(2)}) async-start(), calls=%async_computation.25 | async-start | bytes 2359296 | tf_op jit(solution)/shard_map/reduce_scatter | solution.py:93
  1302.7 5.3 copy-start.8
  1302.7 6.2 copy-start.9
  1318.8 726.9 %reduce-scatter.25.cloned.1.call-start = ((), (), s32[]{:S(2)}) async-start(), calls=%async_computation.24 | async-start | bytes 2359296 | tf_op jit(solution)/shard_map/reduce_scatter | solution.py:93
  1356.7 5.7 copy-start.74
  1356.7 5.7 copy-start.100
  1362.4 6.1 copy-start.57
  1370.7 959.7 %reduce-scatter.31.cloned.1.call-start = ((), (), s32[]{:S(2)}) async-start(), calls=%async_computation.27 | async-start | bytes 18874368 | tf_op jit(solution)/shard_map/reduce_scatter | solution.py:88
  1385.0 1230.7 %reduce-scatter.29.cloned.1.call-start = ((), (), s32[]{:S(2)}) async-start(), calls=%async_computation.26 | async-start | bytes 18874368 | tf_op jit(solution)/shard_map/reduce_scatter | solution.py:88
  1399.5 5.7 copy-start.23
  1417.1 5.6 copy-start.47
  1427.4 479.4 %copy-start.26 = (f32[1,256,2048]{2,1,0:T(8,128)S(1)}, f32[1,256,2048]{2,1,0:T(8,128)}, u32[]{:S(2)}) copy-start(f32[1,256,2048]{2,1,0:T(8,128)} %get-tuple-element.97) | copy-start | bytes 6291460
  2620.9 43.0 %copy-start.29 = (f32[3,256,512]{1,2,0:T(8,128)S(1)}, f32[3,256,512]{1,2,0:T(8,128)}, u32[]{:S(2)}) copy-start(f32[3,256,512]{1,2,0:T(8,128)} %copy.149) | copy-start | bytes 4718596
  2620.9 43.0 %copy-start.30 = (f32[3,256,512]{1,2,0:T(8,128)S(1)}, f32[3,256,512]{1,2,0:T(8,128)}, u32[]{:S(2)}) copy-start(f32[3,256,512]{1,2,0:T(8,128)} %copy.145) | copy-start | bytes 4718596
  2685.0 5.5 copy-start.18
  2685.0 5.5 copy-start.32
  2702.1 5.5 copy-start.21
  2712.5 5.5 copy-start.20
  (76 other events, 171.9 us)
Sparse Core Ops, SparseCore 0:
  10.8 101.7 all-gather.26
  129.0 26.1 all-gather.28
  157.3 27.4 all-gather.38
  187.3 48.7 all-gather.30
  238.1 26.4 all-gather.36
  266.6 27.4 all-gather.44
  296.2 57.7 all-gather.40
  356.1 58.2 all-gather.46
  417.2 227.5 all-gather.32
  647.3 123.0 all-gather.34
  794.6 56.4 all-gather.50
  852.5 58.2 all-gather.54
  935.8 43.8 reduce-scatter.16
  982.6 43.1 reduce-scatter.18
  1027.9 43.1 reduce-scatter.12
  1073.9 43.1 reduce-scatter.14
  1118.6 57.6 all-gather.48
  1178.2 58.2 all-gather.56
  1238.6 58.2 all-gather.52
  1298.4 58.2 all-gather.42
  1360.3 149.3 reduce-scatter.34
  1513.8 148.4 reduce-scatter.32
  1665.9 117.3 reduce-scatter.22
  1786.8 117.5 reduce-scatter.20
  1908.5 66.8 reduce-scatter.26
  1978.8 66.8 reduce-scatter.24
  2049.3 281.0 reduce-scatter.30
  2334.6 281.0 reduce-scatter.28
